TPU v7x, 512 devices: a whole 4x8x8 slice. The times are simulated.
512 devices in a mesh: date: 16 (over z, x_hi), trade: 16 (over y, core), path: 2 (over x_lo).
Axes of the slice: x: 4 (x_hi: 2, x_lo: 2; x = x_hi * 2 + x_lo), y: 8, z: 8, core: 2. Of those that a mesh axis runs over, the one named last changes fastest.
Arguments:
- normals: bfloat16 [32, 64, 8192], P('date', None, ('trade', 'path')), may hold values from -6 to 6
- chol: float32 [64, 64], replicated, as said below
- volatility: float32 [64], replicated, may hold values from 0.5 to 2
- start_state: float32 [64], replicated, may hold values from -3 to 3
- basis_map: float32 [64, 128], replicated, may hold values from -0.75 to 0.75
- basis_bias: float32 [128], replicated, may hold values from -3 to 3
- coef: bfloat16 [128, 16384], P(None, 'trade'), may hold values from -0.5 to 0.5
- maturity: int32 [16384], P('trade'), may hold values from 1 to 32
- netting: int32 [16384], P('trade'), may hold values from 0 to 2047, as said below
Outputs:
- exposure: float32 [32, 2048], P('date', 'trade')
Inputs may be any that keep to these rules, and one draw needn't show every extreme that they name: netting sets are whole within a shard of trades: netting[j] // 128 == j // 1024, and every netting set holds at least one trade. `chol`: lower triangular with a positive diagonal.
All inputs are finite; a program needn't handle non-finite values.
Results may differ from a plain program's by a relative error of at most 0.00035.
Values may be sent and summed in bfloat16 or wider, within the bound.
A program may use at most 64 MiB of HBM per device.

v0:
```python
import jax
import jax.numpy as jnp
from jax import lax
from jax.sharding import PartitionSpec as P

NS_DEV = 128


def entering(array, axis, join, neutral):
    place = lax.axis_index(axis)
    gathered = lax.all_gather(array.astype(jnp.bfloat16), axis)
    state = jnp.zeros_like(array) + jnp.asarray(neutral, array.dtype)

    def one(lap, state):
        return join(state, lax.dynamic_index_in_dim(gathered, lap, 0, False).astype(array.dtype))

    return lax.fori_loop(0, place, one, state)


def add_pair(earlier, later):
    return earlier + later


def local_moves(draws, chol, volatility, date_total):
    scale = volatility * jnp.sqrt(jnp.float32(1.0) / date_total)
    moves = jnp.einsum(
        "fg,tgp->tfp", chol, draws.astype(jnp.float32), precision=lax.Precision.HIGHEST
    )
    return jnp.cumsum(moves * scale[None, :, None], axis=0)


def shards(normals, chol, volatility, start_state, basis_map, basis_bias, coef, maturity, netting):
    date_count, factor_count, path_count = normals.shape
    trade_count = coef.shape[1]
    set_count = trade_count * 0 + NS_DEV
    date_total = date_count * lax.axis_size("date")
    path_total = path_count * lax.axis_size("trade") * lax.axis_size("path")
    first_date = lax.axis_index("date") * date_count
    when = first_date + jnp.arange(date_count, dtype=jnp.int32)
    alive = (when[:, None] < maturity[None, :]).astype(jnp.float32)
    local_set = netting - lax.axis_index("trade") * set_count
    member = (local_set[:, None] == jnp.arange(set_count, dtype=jnp.int32)[None, :]).astype(
        jnp.bfloat16
    )
    own_local = local_moves(normals, chol, volatility, date_total)
    empty = jnp.zeros_like(own_local[-1])
    prior = entering(own_local[-1], "date", add_pair, empty)
    states = start_state[None, :, None] + prior[None] + own_local
    pre = jnp.einsum(
        "tfp,fk->tpk",
        lax.all_gather(states, "trade", axis=2, tiled=True),
        basis_map,
        precision=lax.Precision.HIGHEST,
    )
    basis = jnp.tanh(pre + basis_bias[None, None, :]).astype(jnp.bfloat16)
    value = jnp.einsum("tpk,kj->tpj", basis, coef, preferred_element_type=jnp.float32)
    value = (value * alive[:, None, :]).astype(jnp.bfloat16)
    net = jnp.einsum("tpj,js->tps", value, member, preferred_element_type=jnp.float32)
    total = jnp.sum(jnp.maximum(net, 0.0), axis=1)
    summed = lax.psum(total, "path")
    return summed / path_total


def solution(mesh):
    placed = (
        P("date", None, ("trade", "path")),
        P(),
        P(),
        P(),
        P(),
        P(),
        P(None, "trade"),
        P("trade"),
        P("trade"),
    )
    return jax.shard_map(
        shards, mesh=mesh, in_specs=placed, out_specs=P("date", "trade"), check_vma=False
    )
```

profile of v0, /device:TPU:1, one launch (start us, length us, event | category | flops | bytes accessed | tf_op | source)
XLA Modules:
  0.0 125.8 jit_solution(15111759457493451321)
XLA Ops:
  6.5 0.0 copy-start
  6.5 0.0 copy-start.4
  6.5 0.0 copy-start.3
  6.5 0.0 copy-start.2
  6.5 0.0 copy-start.1
  6.5 0.0 copy-start.5
  6.6 0.0 all-gather.2.cloned.1.call-start
  6.6 0.7 broadcast_multiply_fusion.1
  7.3 1.0 fusion.8
  8.4 0.1 fusion.16
  8.5 43.9 %all_gather.7 = bf16[16,64,256]{2,1,0:T(8,128)(2,1)S(1)} all-gather(bf16[1,64,256]{2,1,0:T(8,128)(2,1)S(1)} %slice.7), channel_id=1, replica_groups=mesh['date'=16,'trade'=16,'path'=2] {'date'}, dimensions={0}, use_global_device_ids=true | all-gather | bytes 557056 | tf_op jit(solution)/shard_map/all_gather | solution.py:11
  52.4 0.0 copy-done.4
  52.4 0.1 broadcast_add_fusion.1
  52.5 0.7 broadcast_add_fusion
  53.2 0.0 all-gather.2.cloned.1.call-update
  53.2 0.0 copy-done.3
  53.2 0.0 copy-done.2
  53.2 0.1 compare_convert_fusion
  53.3 43.9 %all-gather.2.cloned.1.call-done = f32[2,64,4096]{2,1,0:T(8,128)} async-done(((f32[2,64,256]{2,1,0:T(8,128)}), f32[2,64,4096]{2,1,0:T(8,128)}) %all-gather.2.cloned.1.call-update) | async-done | bytes 2097168 | tf_op jit(solution)/shard_map/all_gather | solution.py:51
  97.2 0.0 copy-done.1
  97.2 0.0 copy-done.5
  97.2 8.3 %fusion.6 = bf16[2,4096,128]{2,1,0:T(8,128)(2,1)S(1)} fusion(f32[2,64,4096]{2,1,0:T(8,128)} %all-gather.2.cloned.1.call-done, f32[128]{0:T(128)S(1)} %copy-done.5, f32[64,128]{1,0:T(8,128)S(1)} %copy-done.1), kind=kOutput, calls=%fused_computation.8 | convolution fusion | flops 807403520 | bytes 4227584 | tf_op jit(solution)/shard_map/tfp,fk->tpk/dot_general | solution.py:49
  105.5 0.0 copy-done
  105.5 9.0 %fusion.7 = f32[2,128]{1,0:T(2,128)S(1)} fusion(f32[2,1024]{1,0:T(2,128)S(1)} %compare_convert_fusion, bf16[2,4096,128]{2,1,0:T(8,128)(2,1)S(1)} %fusion.6, bf16[128,1024]{1,0:T(8,128)(2,1)S(1)} %copy-done, s32[1024]{0:T(1024)S(1)} %broadcast_subtract_fusion), kind=kOutput, calls=%fused_computation.9 | convolution fusion | flops 4313972736 | bytes 2372608 | tf_op jit(solution)/shard_map/tpj,js->tps/dot_general | solution.py:58
  114.6 3.8 %psum.7 = f32[2,128]{1,0:T(2,128)S(1)} all-reduce(f32[2,128]{1,0:T(2,128)S(1)} %fusion.7), channel_id=1, replica_groups=mesh['date'=16,'trade'=16,'path'=2] {'path'}, use_global_device_ids=true, to_apply=%region_4.5 | all-reduce | flops 256 | bytes 2048 | tf_op jit(solution)/shard_map/psum | solution.py:60
  118.3 0.6 broadcast_multiply_fusion
  (5 shorter events, 0.0 us)
Async XLA Ops:
  6.5 99.0 %copy-start = (bf16[128,1024]{1,0:T(8,128)(2,1)S(1)}, bf16[128,1024]{1,0:T(8,128)(2,1)}, u32[]{:S(2)}) copy-start(bf16[128,1024]{1,0:T(8,128)(2,1)} %param.17) | copy-start | bytes 786436
  6.5 45.9 %copy-start.4 = (f32[64]{0:T(128)S(1)}, f32[64]{0:T(128)}, u32[]{:S(2)}) copy-start(f32[64]{0:T(128)} %param.14) | copy-start | bytes 772
  6.5 46.7 %copy-start.3 = (s32[1024]{0:T(1024)S(1)}, s32[1024]{0:T(1024)}, u32[]{:S(2)}) copy-start(s32[1024]{0:T(1024)} %param.19) | copy-start | bytes 12292
  6.5 46.7 %copy-start.2 = (s32[1024]{0:T(1024)S(1)}, s32[1024]{0:T(1024)}, u32[]{:S(2)}) copy-start(s32[1024]{0:T(1024)} %param.18) | copy-start | bytes 12292
  6.5 90.6 %copy-start.1 = (f32[64,128]{1,0:T(8,128)S(1)}, f32[64,128]{1,0:T(8,128)}, u32[]{:S(2)}) copy-start(f32[64,128]{1,0:T(8,128)} %param.15) | copy-start | bytes 98308
  6.5 90.6 %copy-start.5 = (f32[128]{0:T(128)S(1)}, f32[128]{0:T(128)}, u32[]{:S(2)}) copy-start(f32[128]{0:T(128)} %param.16) | copy-start | bytes 1540
  6.6 90.6 %all-gather.2.cloned.1.call-start = ((), (), s32[]{:S(2)}) async-start(), calls=%async_computation | async-start | bytes 2228224 | tf_op jit(solution)/shard_map/all_gather | solution.py:51
Sparse Core Ops, SparseCore 0:
  53.3 43.8 all-gather.1
where the time goes:
time: 126 us
  blocking collectives  47.7 us (38%)
  waiting for transfers between devices  43.9 us (35%)
  matrix products  18.4 us (15%)
  between operations  13.5 us (11%)
  other arithmetic  2.22 us (2%)
    all_gather x1, blocking collectives, entering(): gathered = lax.all_gather(array.astype(jnp.bfloat16), axis)  43.9 us
    all_gather x1, waiting for transfers between devices, shards(): lax.all_gather(states, 'trade', axis=2, tiled=True)  43.9 us
    dot_general x1, matrix products, shards(): jnp.einsum('tpj,js->tps', value, member, preferred_element_type=jnp.float32)  9.03 us
    dot_general x1, matrix products, shards(): jnp.einsum('tfp,fk->tpk', lax.all_gather(states, 'trade', axis=2, tiled=T...  8.32 us
    psum x1, blocking collectives, shards(): summed = lax.psum(total, 'path')  3.79 us
  transfers between devices with their start and end apart: 1, of which 1 were waited for; matrix products, arithmetic and copies ran while one was open for 0% of the time, Pallas kernels for 0%

commit v1 on v0

--- a/solution.py
+++ b/solution.py
@@ -4,6 +4,20 @@
 from jax.sharding import PartitionSpec as P
 
 NS_DEV = 128
+
+
+def on_each_block(x, axis, dim, make, out_dim):
+    ways, here, step = (lax.axis_size(axis), lax.axis_index(axis), x.shape[dim])
+    earlier, later = ([], [])
+    going_up = going_down = x
+    for far in range(ways // 2 + 1):
+        earlier.append(make(going_up, (here - far) % ways * step))
+        if 0 < far < ways - ways // 2:
+            later.append(make(going_down, (here + far) % ways * step))
+        going_up = lax.ppermute(going_up, axis, [(d, (d + 1) % ways) for d in range(ways)])
+        going_down = lax.ppermute(going_down, axis, [(d, (d - 1) % ways) for d in range(ways)])
+    line = jnp.concatenate([*earlier[::-1], *later], axis=out_dim)
+    return jnp.roll(line, (here - ways // 2) * earlier[0].shape[out_dim], axis=out_dim)
 
 
 def entering(array, axis, join, neutral):
@@ -46,11 +60,14 @@
     empty = jnp.zeros_like(own_local[-1])
     prior = entering(own_local[-1], "date", add_pair, empty)
     states = start_state[None, :, None] + prior[None] + own_local
-    pre = jnp.einsum(
-        "tfp,fk->tpk",
-        lax.all_gather(states, "trade", axis=2, tiled=True),
-        basis_map,
-        precision=lax.Precision.HIGHEST,
+    pre = on_each_block(
+        states,
+        "trade",
+        2,
+        lambda shard, offset: jnp.einsum(
+            "tfp,fk->tpk", shard, basis_map, precision=lax.Precision.HIGHEST
+        ),
+        1,
     )
     basis = jnp.tanh(pre + basis_bias[None, None, :]).astype(jnp.bfloat16)
     value = jnp.einsum("tpk,kj->tpj", basis, coef, preferred_element_type=jnp.float32)

time: 126 us -> 154 us (1.22)
  the two profiles are of different devices: /device:TPU:1 before, /device:TPU:32 now
where the time goes in v1:
time: 154 us; the launch traced here: 153 us
  blocking collectives  54.8 us (36%)
  matrix products  40.1 us (26%)
  waiting for transfers between devices  22.6 us (15%)
  starting transfers between devices  20.8 us (14%)
  local copies, waits for them, and re-layouts  11.5 us (7%)
  other arithmetic  3.58 us (2%)
    all_gather x1, blocking collectives, entering(): gathered = lax.all_gather(array.astype(jnp.bfloat16), axis)  49.8 us
    dot_general x16, matrix products, shards(): jnp.einsum('tfp,fk->tpk', shard, basis_map, precision=lax.Precision.HIGHEST)  27.6 us
    ppermute x8, waiting for transfers between devices, on_each_block(): lax.ppermute(going_up, axis, [(d, (d + 1) % ways) for d in range(ways)])  22.6 us
    ppermute x7, starting transfers between devices, on_each_block(): lax.ppermute(going_down, axis, [(d, (d - 1) % ways) for d in range(ways)])  20.7 us
    dot_general x1, matrix products, shards(): jnp.einsum('tpj,js->tps', value, member, preferred_element_type=jnp.float32)  11.4 us
    unnamed x21, local copies, waits for them, and re-layouts  10.8 us
    psum x1, blocking collectives, shards(): summed = lax.psum(total, 'path')  4.94 us
  transfers between devices with their start and end apart: 15, of which 8 were waited for; matrix products, arithmetic and copies ran while one was open for 18% of the time, Pallas kernels for 0%

profile of v1, /device:TPU:32, one launch (start us, length us, event | category | flops | bytes accessed | tf_op | source)
XLA Modules:
  0.0 153.4 jit_solution(4039722062248073170)
XLA Ops:
  1.9 49.8 %all_gather.4 = bf16[16,64,256]{2,1,0:T(8,128)(2,1)S(1)} all-gather(bf16[1,64,256]{2,1,0:T(8,128)(2,1)S(1)} %slice.7), channel_id=1, replica_groups=mesh['date'=16,'trade'=16,'path'=2] {'date'}, dimensions={0}, use_global_device_ids=true | all-gather | bytes 557056 | tf_op jit(solution)/shard_map/all_gather | solution.py:25
  52.5 5.6 %collective-permute-done = f32[2,64,256]{2,1,0:T(8,128)S(1)} collective-permute-done((f32[2,64,256]{2,1,0:T(8,128)S(1)}, f32[2,64,256]{2,1,0:T(8,128)S(1)}, u32[]{:S(2)}, u32[]{:S(2)}) %collective-permute-start) | collective-permute-done | bytes 131104 | tf_op jit(solution)/shard_map/ppermute | solution.py:17
  58.1 3.0 %collective-permute-start.8 = (f32[2,64,256]{2,1,0:T(8,128)S(1)}, f32[2,64,256]{2,1,0:T(8,128)S(1)}, u32[]{:S(2)}, u32[]{:S(2)}) collective-permute-start(f32[2,64,256]{2,1,0:T(8,128)S(1)} %broadcast_add_fusion), channel_id=1, source_target_pairs={{0,30},{2,0},{4,2},{6,4},{8,6},{10,8},{12,10},{14,12},{16,14},{18,... | collective-permute-start | bytes 393224 | tf_op jit(solution)/shard_map/ppermute | solution.py:18
  61.0 2.6 %collective-permute-done.1 = f32[2,64,256]{2,1,0:T(8,128)S(1)} collective-permute-done((f32[2,64,256]{2,1,0:T(8,128)S(1)}, f32[2,64,256]{2,1,0:T(8,128)S(1)}, u32[]{:S(2)}, u32[]{:S(2)}) %collective-permute-start.1) | collective-permute-done | bytes 131104 | tf_op jit(solution)/shard_map/ppermute | solution.py:17
  63.7 3.0 %collective-permute-start.9 = (f32[2,64,256]{2,1,0:T(8,128)S(1)}, f32[2,64,256]{2,1,0:T(8,128)S(1)}, u32[]{:S(2)}, u32[]{:S(2)}) collective-permute-start(f32[2,64,256]{2,1,0:T(8,128)S(1)} %collective-permute-done.8), channel_id=1, source_target_pairs={{0,30},{2,0},{4,2},{6,4},{8,6},{10,8},{12,10},{14,12},{16,14},{18,... | collective-permute-start | bytes 393224 | tf_op jit(solution)/shard_map/ppermute | solution.py:18
  66.7 2.6 %collective-permute-done.2 = f32[2,64,256]{2,1,0:T(8,128)S(1)} collective-permute-done((f32[2,64,256]{2,1,0:T(8,128)S(1)}, f32[2,64,256]{2,1,0:T(8,128)S(1)}, u32[]{:S(2)}, u32[]{:S(2)}) %collective-permute-start.2) | collective-permute-done | bytes 131104 | tf_op jit(solution)/shard_map/ppermute | solution.py:17
  69.3 3.0 %collective-permute-start.10 = (f32[2,64,256]{2,1,0:T(8,128)S(1)}, f32[2,64,256]{2,1,0:T(8,128)S(1)}, u32[]{:S(2)}, u32[]{:S(2)}) collective-permute-start(f32[2,64,256]{2,1,0:T(8,128)S(1)} %collective-permute-done.9), channel_id=1, source_target_pairs={{0,30},{2,0},{4,2},{6,4},{8,6},{10,8},{12,10},{14,12},{16,14},{18,... | collective-permute-start | bytes 393224 | tf_op jit(solution)/shard_map/ppermute | solution.py:18
  72.3 2.6 %collective-permute-done.3 = f32[2,64,256]{2,1,0:T(8,128)S(1)} collective-permute-done((f32[2,64,256]{2,1,0:T(8,128)S(1)}, f32[2,64,256]{2,1,0:T(8,128)S(1)}, u32[]{:S(2)}, u32[]{:S(2)}) %collective-permute-start.3) | collective-permute-done | bytes 131104 | tf_op jit(solution)/shard_map/ppermute | solution.py:17
  74.9 3.0 %collective-permute-start.11 = (f32[2,64,256]{2,1,0:T(8,128)S(1)}, f32[2,64,256]{2,1,0:T(8,128)S(1)}, u32[]{:S(2)}, u32[]{:S(2)}) collective-permute-start(f32[2,64,256]{2,1,0:T(8,128)S(1)} %collective-permute-done.10), channel_id=1, source_target_pairs={{0,30},{2,0},{4,2},{6,4},{8,6},{10,8},{12,10},{14,12},{16,14},{18,... | collective-permute-start | bytes 393224 | tf_op jit(solution)/shard_map/ppermute | solution.py:18
  77.9 2.6 %collective-permute-done.4 = f32[2,64,256]{2,1,0:T(8,128)S(1)} collective-permute-done((f32[2,64,256]{2,1,0:T(8,128)S(1)}, f32[2,64,256]{2,1,0:T(8,128)S(1)}, u32[]{:S(2)}, u32[]{:S(2)}) %collective-permute-start.4) | collective-permute-done | bytes 131104 | tf_op jit(solution)/shard_map/ppermute | solution.py:17
  80.5 3.0 %collective-permute-start.12 = (f32[2,64,256]{2,1,0:T(8,128)S(1)}, f32[2,64,256]{2,1,0:T(8,128)S(1)}, u32[]{:S(2)}, u32[]{:S(2)}) collective-permute-start(f32[2,64,256]{2,1,0:T(8,128)S(1)} %collective-permute-done.11), channel_id=1, source_target_pairs={{0,30},{2,0},{4,2},{6,4},{8,6},{10,8},{12,10},{14,12},{16,14},{18,... | collective-permute-start | bytes 393224 | tf_op jit(solution)/shard_map/ppermute | solution.py:18
  83.5 2.6 %collective-permute-done.5 = f32[2,64,256]{2,1,0:T(8,128)S(1)} collective-permute-done((f32[2,64,256]{2,1,0:T(8,128)S(1)}, f32[2,64,256]{2,1,0:T(8,128)S(1)}, u32[]{:S(2)}, u32[]{:S(2)}) %collective-permute-start.5) | collective-permute-done | bytes 131104 | tf_op jit(solution)/shard_map/ppermute | solution.py:17
  86.9 3.0 %collective-permute-start.13 = (f32[2,64,256]{2,1,0:T(8,128)S(1)}, f32[2,64,256]{2,1,0:T(8,128)S(1)}, u32[]{:S(2)}, u32[]{:S(2)}) collective-permute-start(f32[2,64,256]{2,1,0:T(8,128)S(1)} %collective-permute-done.12), channel_id=1, source_target_pairs={{0,30},{2,0},{4,2},{6,4},{8,6},{10,8},{12,10},{14,12},{16,14},{18,... | collective-permute-start | bytes 393224 | tf_op jit(solution)/shard_map/ppermute | solution.py:18
  89.8 1.9 %collective-permute-done.6 = f32[2,64,256]{2,1,0:T(8,128)S(1)} collective-permute-done((f32[2,64,256]{2,1,0:T(8,128)S(1)}, f32[2,64,256]{2,1,0:T(8,128)S(1)}, u32[]{:S(2)}, u32[]{:S(2)}) %collective-permute-start.6) | collective-permute-done | bytes 131104 | tf_op jit(solution)/shard_map/ppermute | solution.py:17
  92.4 3.0 %collective-permute-start.14 = (f32[2,64,256]{2,1,0:T(8,128)S(1)}, f32[2,64,256]{2,1,0:T(8,128)S(1)}, u32[]{:S(2)}, u32[]{:S(2)}) collective-permute-start(f32[2,64,256]{2,1,0:T(8,128)S(1)} %collective-permute-done.13), channel_id=1, source_target_pairs={{0,30},{2,0},{4,2},{6,4},{8,6},{10,8},{12,10},{14,12},{16,14},{18,... | collective-permute-start | bytes 393224 | tf_op jit(solution)/shard_map/ppermute | solution.py:18
  95.4 1.9 %collective-permute-done.7 = f32[2,64,256]{2,1,0:T(8,128)S(1)} collective-permute-done((f32[2,64,256]{2,1,0:T(8,128)S(1)}, f32[2,64,256]{2,1,0:T(8,128)S(1)}, u32[]{:S(2)}, u32[]{:S(2)}) %collective-permute-start.7) | collective-permute-done | bytes 131104 | tf_op jit(solution)/shard_map/ppermute | solution.py:17
  97.3 2.1 %constant_dynamic-update-slice_fusion.31 = (f32[2,8192,128]{2,1,0:T(8,128)}, f32[2,256,128]{2,1,0:T(8,128)S(1)}) fusion(f32[2,64,256]{2,1,0:T(8,128)S(1)} %collective-permute-done.7, f32[64,128]{1,0:T(8,128)} %param.15), kind=kOutput, calls=%fused_computation.46 | convolution fusion | flops 50331648 | bytes 688128 | tf_op jit(solution)/shard_map/tfp,fk->tpk/dot_general | solution.py:67
  99.4 2.0 %constant_dynamic-update-slice_fusion.30 = (f32[2,8192,128]{2,1,0:T(8,128)}, f32[2,256,128]{2,1,0:T(8,128)S(1)}) fusion(f32[2,8192,128]{2,1,0:T(8,128)} %get-tuple-element.37, f32[2,64,256]{2,1,0:T(8,128)S(1)} %collective-permute-done.6, f32[64,128]{1,0:T(8,128)} %param.15), kind=kOutput, calls=%fused_computation.45 | convolution fusion | flops 50331648 | bytes 688128 | tf_op jit(solution)/shard_map/tfp,fk->tpk/dot_general | solution.py:67
  101.4 2.0 %constant_dynamic-update-slice_fusion.29 = (f32[2,8192,128]{2,1,0:T(8,128)}, f32[2,256,128]{2,1,0:T(8,128)S(1)}) fusion(f32[2,8192,128]{2,1,0:T(8,128)} %get-tuple-element.39, f32[2,64,256]{2,1,0:T(8,128)S(1)} %collective-permute-done.5, f32[64,128]{1,0:T(8,128)} %param.15), kind=kOutput, calls=%fused_computation.44 | convolution fusion | flops 50331648 | bytes 688128 | tf_op jit(solution)/shard_map/tfp,fk->tpk/dot_general | solution.py:67
  103.5 2.1 %constant_dynamic-update-slice_fusion.28 = (f32[2,8192,128]{2,1,0:T(8,128)}, f32[2,256,128]{2,1,0:T(8,128)S(1)}) fusion(f32[2,8192,128]{2,1,0:T(8,128)} %get-tuple-element.41, f32[2,64,256]{2,1,0:T(8,128)S(1)} %collective-permute-done.4, f32[64,128]{1,0:T(8,128)} %param.15), kind=kOutput, calls=%fused_computation.43 | convolution fusion | flops 50331648 | bytes 688128 | tf_op jit(solution)/shard_map/tfp,fk->tpk/dot_general | solution.py:67
  105.5 2.1 %constant_dynamic-update-slice_fusion.27 = (f32[2,8192,128]{2,1,0:T(8,128)}, f32[2,256,128]{2,1,0:T(8,128)S(1)}) fusion(f32[2,8192,128]{2,1,0:T(8,128)} %get-tuple-element.43, f32[2,64,256]{2,1,0:T(8,128)S(1)} %collective-permute-done.3, f32[64,128]{1,0:T(8,128)} %param.15), kind=kOutput, calls=%fused_computation.42 | convolution fusion | flops 50331648 | bytes 688128 | tf_op jit(solution)/shard_map/tfp,fk->tpk/dot_general | solution.py:67
  107.6 2.1 %constant_dynamic-update-slice_fusion.26 = (f32[2,8192,128]{2,1,0:T(8,128)}, f32[2,256,128]{2,1,0:T(8,128)S(1)}) fusion(f32[2,8192,128]{2,1,0:T(8,128)} %get-tuple-element.45, f32[2,64,256]{2,1,0:T(8,128)S(1)} %collective-permute-done.2, f32[64,128]{1,0:T(8,128)} %param.15), kind=kOutput, calls=%fused_computation.41 | convolution fusion | flops 50331648 | bytes 688128 | tf_op jit(solution)/shard_map/tfp,fk->tpk/dot_general | solution.py:67
  109.7 2.1 %constant_dynamic-update-slice_fusion.25 = (f32[2,8192,128]{2,1,0:T(8,128)}, f32[2,256,128]{2,1,0:T(8,128)S(1)}) fusion(f32[2,8192,128]{2,1,0:T(8,128)} %get-tuple-element.47, f32[2,64,256]{2,1,0:T(8,128)S(1)} %collective-permute-done.1, f32[64,128]{1,0:T(8,128)} %param.15), kind=kOutput, calls=%fused_computation.40 | convolution fusion | flops 50331648 | bytes 688128 | tf_op jit(solution)/shard_map/tfp,fk->tpk/dot_general | solution.py:67
  111.7 2.1 %constant_dynamic-update-slice_fusion.24 = (f32[2,8192,128]{2,1,0:T(8,128)}, f32[2,256,128]{2,1,0:T(8,128)S(1)}) fusion(f32[2,8192,128]{2,1,0:T(8,128)} %get-tuple-element.49, f32[2,64,256]{2,1,0:T(8,128)S(1)} %collective-permute-done, f32[64,128]{1,0:T(8,128)} %param.15), kind=kOutput, calls=%fused_computation.39 | convolution fusion | flops 50331648 | bytes 688128 | tf_op jit(solution)/shard_map/tfp,fk->tpk/dot_general | solution.py:67
  113.8 2.1 %constant_dynamic-update-slice_fusion.23 = (f32[2,8192,128]{2,1,0:T(8,128)}, f32[2,256,128]{2,1,0:T(8,128)S(1)}) fusion(f32[2,8192,128]{2,1,0:T(8,128)} %get-tuple-element.51, f32[2,64,256]{2,1,0:T(8,128)S(1)} %broadcast_add_fusion, f32[64,128]{1,0:T(8,128)} %param.15), kind=kOutput, calls=%fused_computation.38 | convolution fusion | flops 50331648 | bytes 688128 | tf_op jit(solution)/shard_map/tfp,fk->tpk/dot_general | solution.py:67
  115.8 1.3 constant_dynamic-update-slice_fusion.22
  117.1 1.3 constant_dynamic-update-slice_fusion.21
  118.4 1.3 constant_dynamic-update-slice_fusion.20
  121.1 1.3 constant_dynamic-update-slice_fusion.18
  122.4 1.3 constant_dynamic-update-slice_fusion.17
  136.5 11.4 %fusion.7 = f32[2,128]{1,0:T(2,128)S(1)} fusion(f32[2,1024]{1,0:T(2,128)S(1)} %compare_convert_fusion, f32[2,8192,128]{2,1,0:T(8,128)} %constant_dynamic-update-slice_fusion, s32[]{:T(128)S(6)} %select_n.18, f32[128]{0:T(128)S(1)} %copy-done.2, bf16[128,1024]{1,0:T(8,128)(2,1)S(1)} %copy-done, s32[1024]{0:T(1024)S(1)} %broadcast_subtract_fusion), kind=kOutput, calls=%fused_computation.8 | convolution fusion | flops 4316069888 | bytes 4470276 | tf_op jit(solution)/shard_map/tpj,js->tps/dot_general | solution.py:75
  147.9 4.9 %psum.7 = f32[2,128]{1,0:T(2,128)S(1)} all-reduce(f32[2,128]{1,0:T(2,128)S(1)} %fusion.7), channel_id=1, replica_groups=mesh['date'=16,'trade'=16,'path'=2] {'path'}, use_global_device_ids=true, to_apply=%region_4.5 | all-reduce | flops 256 | bytes 2048 | tf_op jit(solution)/shard_map/psum | solution.py:77
  (51 shorter events, 18.8 us)
Async XLA Ops:
  0.0 136.5 %copy-start = (bf16[128,1024]{1,0:T(8,128)(2,1)S(1)}, bf16[128,1024]{1,0:T(8,128)(2,1)}, u32[]{:S(2)}) copy-start(bf16[128,1024]{1,0:T(8,128)(2,1)} %param.17) | copy-start | bytes 786436
  0.0 115.8 %copy-start.1 = (f32[64,128]{1,0:T(8,128)S(1)}, f32[64,128]{1,0:T(8,128)}, u32[]{:S(2)}) copy-start(f32[64,128]{1,0:T(8,128)} %param.15) | copy-start | bytes 98308
  52.5 5.6 %collective-permute-start = (f32[2,64,256]{2,1,0:T(8,128)S(1)}, f32[2,64,256]{2,1,0:T(8,128)S(1)}, u32[]{:S(2)}, u32[]{:S(2)}) collective-permute-start(f32[2,64,256]{2,1,0:T(8,128)S(1)} %broadcast_add_fusion), channel_id=1, source_target_pairs={{0,2},{2,4},{4,6},{6,8},{8,10},{10,12},{12,14},{14,16},{16,18},{18... | collective-permute-start | bytes 393224 | tf_op jit(solution)/shard_map/ppermute | solution.py:17
  58.1 5.6 %collective-permute-start.1 = (f32[2,64,256]{2,1,0:T(8,128)S(1)}, f32[2,64,256]{2,1,0:T(8,128)S(1)}, u32[]{:S(2)}, u32[]{:S(2)}) collective-permute-start(f32[2,64,256]{2,1,0:T(8,128)S(1)} %collective-permute-done), channel_id=1, source_target_pairs={{0,2},{2,4},{4,6},{6,8},{8,10},{10,12},{12,14},{14,16},{16,18},{18... | collective-permute-start | bytes 393224 | tf_op jit(solution)/shard_map/ppermute | solution.py:17
  58.1 5.6 %collective-permute-start.8 = (f32[2,64,256]{2,1,0:T(8,128)S(1)}, f32[2,64,256]{2,1,0:T(8,128)S(1)}, u32[]{:S(2)}, u32[]{:S(2)}) collective-permute-start(f32[2,64,256]{2,1,0:T(8,128)S(1)} %broadcast_add_fusion), channel_id=1, source_target_pairs={{0,30},{2,0},{4,2},{6,4},{8,6},{10,8},{12,10},{14,12},{16,14},{18,... | collective-permute-start | bytes 393224 | tf_op jit(solution)/shard_map/ppermute | solution.py:18
  63.7 5.6 %collective-permute-start.2 = (f32[2,64,256]{2,1,0:T(8,128)S(1)}, f32[2,64,256]{2,1,0:T(8,128)S(1)}, u32[]{:S(2)}, u32[]{:S(2)}) collective-permute-start(f32[2,64,256]{2,1,0:T(8,128)S(1)} %collective-permute-done.1), channel_id=1, source_target_pairs={{0,2},{2,4},{4,6},{6,8},{8,10},{10,12},{12,14},{14,16},{16,18},{18... | collective-permute-start | bytes 393224 | tf_op jit(solution)/shard_map/ppermute | solution.py:17
  63.7 5.6 %collective-permute-start.9 = (f32[2,64,256]{2,1,0:T(8,128)S(1)}, f32[2,64,256]{2,1,0:T(8,128)S(1)}, u32[]{:S(2)}, u32[]{:S(2)}) collective-permute-start(f32[2,64,256]{2,1,0:T(8,128)S(1)} %collective-permute-done.8), channel_id=1, source_target_pairs={{0,30},{2,0},{4,2},{6,4},{8,6},{10,8},{12,10},{14,12},{16,14},{18,... | collective-permute-start | bytes 393224 | tf_op jit(solution)/shard_map/ppermute | solution.py:18
  69.3 5.6 %collective-permute-start.3 = (f32[2,64,256]{2,1,0:T(8,128)S(1)}, f32[2,64,256]{2,1,0:T(8,128)S(1)}, u32[]{:S(2)}, u32[]{:S(2)}) collective-permute-start(f32[2,64,256]{2,1,0:T(8,128)S(1)} %collective-permute-done.2), channel_id=1, source_target_pairs={{0,2},{2,4},{4,6},{6,8},{8,10},{10,12},{12,14},{14,16},{16,18},{18... | collective-permute-start | bytes 393224 | tf_op jit(solution)/shard_map/ppermute | solution.py:17
  69.3 5.6 %collective-permute-start.10 = (f32[2,64,256]{2,1,0:T(8,128)S(1)}, f32[2,64,256]{2,1,0:T(8,128)S(1)}, u32[]{:S(2)}, u32[]{:S(2)}) collective-permute-start(f32[2,64,256]{2,1,0:T(8,128)S(1)} %collective-permute-done.9), channel_id=1, source_target_pairs={{0,30},{2,0},{4,2},{6,4},{8,6},{10,8},{12,10},{14,12},{16,14},{18,... | collective-permute-start | bytes 393224 | tf_op jit(solution)/shard_map/ppermute | solution.py:18
  74.9 5.6 %collective-permute-start.4 = (f32[2,64,256]{2,1,0:T(8,128)S(1)}, f32[2,64,256]{2,1,0:T(8,128)S(1)}, u32[]{:S(2)}, u32[]{:S(2)}) collective-permute-start(f32[2,64,256]{2,1,0:T(8,128)S(1)} %collective-permute-done.3), channel_id=1, source_target_pairs={{0,2},{2,4},{4,6},{6,8},{8,10},{10,12},{12,14},{14,16},{16,18},{18... | collective-permute-start | bytes 393224 | tf_op jit(solution)/shard_map/ppermute | solution.py:17
  74.9 5.6 %collective-permute-start.11 = (f32[2,64,256]{2,1,0:T(8,128)S(1)}, f32[2,64,256]{2,1,0:T(8,128)S(1)}, u32[]{:S(2)}, u32[]{:S(2)}) collective-permute-start(f32[2,64,256]{2,1,0:T(8,128)S(1)} %collective-permute-done.10), channel_id=1, source_target_pairs={{0,30},{2,0},{4,2},{6,4},{8,6},{10,8},{12,10},{14,12},{16,14},{18,... | collective-permute-start | bytes 393224 | tf_op jit(solution)/shard_map/ppermute | solution.py:18
  80.5 5.6 %collective-permute-start.5 = (f32[2,64,256]{2,1,0:T(8,128)S(1)}, f32[2,64,256]{2,1,0:T(8,128)S(1)}, u32[]{:S(2)}, u32[]{:S(2)}) collective-permute-start(f32[2,64,256]{2,1,0:T(8,128)S(1)} %collective-permute-done.4), channel_id=1, source_target_pairs={{0,2},{2,4},{4,6},{6,8},{8,10},{10,12},{12,14},{14,16},{16,18},{18... | collective-permute-start | bytes 393224 | tf_op jit(solution)/shard_map/ppermute | solution.py:17
  80.5 6.4 %collective-permute-start.12 = (f32[2,64,256]{2,1,0:T(8,128)S(1)}, f32[2,64,256]{2,1,0:T(8,128)S(1)}, u32[]{:S(2)}, u32[]{:S(2)}) collective-permute-start(f32[2,64,256]{2,1,0:T(8,128)S(1)} %collective-permute-done.11), channel_id=1, source_target_pairs={{0,30},{2,0},{4,2},{6,4},{8,6},{10,8},{12,10},{14,12},{16,14},{18,... | collective-permute-start | bytes 393224 | tf_op jit(solution)/shard_map/ppermute | solution.py:18
  86.1 5.6 %collective-permute-start.6 = (f32[2,64,256]{2,1,0:T(8,128)S(1)}, f32[2,64,256]{2,1,0:T(8,128)S(1)}, u32[]{:S(2)}, u32[]{:S(2)}) collective-permute-start(f32[2,64,256]{2,1,0:T(8,128)S(1)} %collective-permute-done.5), channel_id=1, source_target_pairs={{0,2},{2,4},{4,6},{6,8},{8,10},{10,12},{12,14},{14,16},{16,18},{18... | collective-permute-start | bytes 393224 | tf_op jit(solution)/shard_map/ppermute | solution.py:17
  86.9 5.5 %collective-permute-start.13 = (f32[2,64,256]{2,1,0:T(8,128)S(1)}, f32[2,64,256]{2,1,0:T(8,128)S(1)}, u32[]{:S(2)}, u32[]{:S(2)}) collective-permute-start(f32[2,64,256]{2,1,0:T(8,128)S(1)} %collective-permute-done.12), channel_id=1, source_target_pairs={{0,30},{2,0},{4,2},{6,4},{8,6},{10,8},{12,10},{14,12},{16,14},{18,... | collective-permute-start | bytes 393224 | tf_op jit(solution)/shard_map/ppermute | solution.py:18
  91.7 5.6 %collective-permute-start.7 = (f32[2,64,256]{2,1,0:T(8,128)S(1)}, f32[2,64,256]{2,1,0:T(8,128)S(1)}, u32[]{:S(2)}, u32[]{:S(2)}) collective-permute-start(f32[2,64,256]{2,1,0:T(8,128)S(1)} %collective-permute-done.6), channel_id=1, source_target_pairs={{0,2},{2,4},{4,6},{6,8},{8,10},{10,12},{12,14},{14,16},{16,18},{18... | collective-permute-start | bytes 393224 | tf_op jit(solution)/shard_map/ppermute | solution.py:17
  92.4 31.3 %collective-permute-start.14 = (f32[2,64,256]{2,1,0:T(8,128)S(1)}, f32[2,64,256]{2,1,0:T(8,128)S(1)}, u32[]{:S(2)}, u32[]{:S(2)}) collective-permute-start(f32[2,64,256]{2,1,0:T(8,128)S(1)} %collective-permute-done.13), channel_id=1, source_target_pairs={{0,30},{2,0},{4,2},{6,4},{8,6},{10,8},{12,10},{14,12},{16,14},{18,... | collective-permute-start | bytes 393224 | tf_op jit(solution)/shard_map/ppermute | solution.py:18
  105.5 31.0 %copy-start.2 = (f32[128]{0:T(128)S(1)}, f32[128]{0:T(128)}, u32[]{:S(2)}) copy-start(f32[128]{0:T(128)} %param.16) | copy-start | bytes 1540
